TPU v7x, 32 devices: a whole 2x2x4 slice. The times are simulated.
32 devices in a mesh: dp: 8 (over z, x), seq: 4 (over y, core).
Axes of the slice: x: 2, y: 2, z: 4, core: 2. Of those that a mesh axis runs over, the one named last changes fastest.
Arguments:
- inputs: bfloat16 [32, 1024, 1024], P('dp', 'seq'), may hold values from -6 to 6
- norm_gain: float32 [1024], replicated, may hold values from 0.1 to 1.9
- norm_shift: float32 [1024], replicated, may hold values from -3 to 3
- qkv_weight: bfloat16 [1024, 3072], replicated, may hold values from -0.1875 to 0.1875
- out_weight: bfloat16 [1024, 1024], replicated, may hold values from -0.75 to 0.75
- up_weight: bfloat16 [1024, 4096], replicated, may hold values from -0.1875 to 0.1875
- up_bias: float32 [4096], replicated, may hold values from -3 to 3
- down_weight: bfloat16 [4096, 1024], replicated, may hold values from -0.09375 to 0.09375
- down_bias: float32 [1024], replicated, may hold values from -3 to 3
- partners: int32 [32], P('dp'), may hold values from 0 to 31, as said below
- families: int32 [32, 1024], P('dp'), may hold values from 0 to 1023, as said below
- cotangent: bfloat16 [32, 1024, 1024], P('dp', 'seq'), may hold values from -6 to 6
Outputs:
- layer_out: bfloat16 [32, 1024, 1024], P('dp', 'seq')
- input_grad: float32 [32, 1024, 1024], P('dp', 'seq')
- gain_grad: float32 [1024], replicated
- shift_grad: float32 [1024], replicated
- qkv_grad: float32 [1024, 3072], P('dp', 'seq')
- out_grad: float32 [1024, 1024], P('dp', 'seq')
- up_grad: float32 [1024, 4096], P('dp', 'seq')
- up_bias_grad: float32 [4096], replicated
- down_grad: float32 [4096, 1024], P('dp', 'seq')
- down_bias_grad: float32 [1024], replicated
Inputs may be any that keep to these rules, and one draw needn't show every extreme that they name: partners pairs the rows of each aligned block of 4 rows two by two: partners[partners[r]] = r, partners[r] != r, and partners[r] lies in the block of r. `families`: family ids never fall along a row and the last position of every row has id 1024 - 1; in each aligned block of 4 rows at least one row is a single group over all 1024 positions.
All inputs are finite; a program needn't handle non-finite values.
Results may differ from a plain program's by a relative error of at most 0.0099.
Values may be sent and summed in bfloat16 or wider, within the bound.
A program may use at most 256 MiB of HBM per device.

v0:
```python
import jax
import jax.numpy as jnp
from jax import lax
from jax.sharding import PartitionSpec as P

HEADS = 16
HEAD_DIM = 64
ROT = 32
EPS = 1e-05


def norm_piece(values, norm_gain, norm_shift):
    row_mean = jnp.mean(values, -1, keepdims=True)
    centered = values - row_mean
    variance = jnp.mean(centered * centered, -1, keepdims=True)
    return centered * lax.rsqrt(variance + EPS) * norm_gain + norm_shift


def rotate(values, places):
    half_rot = ROT // 2
    inverse_freq = 10000.0 ** (-2.0 * jnp.arange(half_rot).astype(jnp.float32) / ROT)
    angles = places.astype(jnp.float32)[:, None] * inverse_freq[None, :]
    cosine_table = jnp.cos(angles)[:, None, :]
    sine_table = jnp.sin(angles)[:, None, :]
    first_half = values[..., :half_rot]
    second_half = values[..., half_rot:ROT]
    return jnp.concatenate(
        [
            first_half * cosine_table - second_half * sine_table,
            second_half * cosine_table + first_half * sine_table,
            values[..., ROT:],
        ],
        -1,
    )


def gelu_piece(values):
    return jax.nn.gelu(values, approximate=True)


def masked_scores(queries, key_rows, family):
    scaling = HEAD_DIM ** (-0.5)
    scores = (
        jnp.einsum("qhd,khd->hqk", queries, key_rows, preferred_element_type=jnp.float32) * scaling
    )
    places = jnp.arange(queries.shape[0])
    allowed = (places[None, :] <= places[:, None]) & (family[:, None] == family[None, :])
    return jnp.where(allowed[None], scores, -1000000000.0)


def forward_row(pieces):
    qkv_rows, family = pieces
    scores = masked_scores(qkv_rows[:, 0], qkv_rows[:, 1], family)
    row_max = jnp.max(scores, -1, keepdims=True)
    weights = jnp.exp(scores - row_max)
    row_total = jnp.sum(weights, -1, keepdims=True)
    prob_low = (weights / row_total).astype(jnp.bfloat16)
    mixed_heads = jnp.einsum(
        "hqk,khd->qhd", prob_low, qkv_rows[:, 2], preferred_element_type=jnp.float32
    )
    return (mixed_heads.astype(jnp.bfloat16), (row_max + jnp.log(row_total))[..., 0])


def backward_row(pieces):
    qkv_rows, family, log_total, d_mixed = pieces
    scaling = HEAD_DIM ** (-0.5)
    queries = qkv_rows[:, 0]
    key_rows = qkv_rows[:, 1]
    value_rows = qkv_rows[:, 2]
    scores = masked_scores(queries, key_rows, family)
    chances = jnp.exp(scores - log_total[..., None])
    d_chances = jnp.einsum("qhd,khd->hqk", d_mixed, value_rows, preferred_element_type=jnp.float32)
    d_scores = (chances * (d_chances - jnp.sum(chances * d_chances, -1, keepdims=True))).astype(
        jnp.bfloat16
    )
    d_value = jnp.einsum(
        "hqk,qhd->khd", chances.astype(jnp.bfloat16), d_mixed, preferred_element_type=jnp.float32
    )
    d_query = (
        jnp.einsum("hqk,khd->qhd", d_scores, key_rows, preferred_element_type=jnp.float32) * scaling
    )
    d_key = (
        jnp.einsum("hqk,qhd->khd", d_scores, queries, preferred_element_type=jnp.float32) * scaling
    )
    return jnp.stack([d_query, d_key, d_value], 1).astype(jnp.bfloat16)


def on_device(
    inputs,
    norm_gain,
    norm_shift,
    qkv_weight,
    out_weight,
    up_weight,
    up_bias,
    down_weight,
    down_bias,
    partners,
    families,
    cotangent,
):
    row_count, place_count, model_width = inputs.shape
    seq_size = lax.axis_size("seq")
    token_count = row_count * place_count
    values = inputs.astype(jnp.float32)
    normed, norm_pull = jax.vjp(norm_piece, values, norm_gain, norm_shift)
    normed_low = normed.astype(jnp.bfloat16).reshape(token_count, model_width)
    raw_qkv = jnp.dot(normed_low, qkv_weight, preferred_element_type=jnp.float32)
    raw_qkv = raw_qkv.reshape(row_count, place_count, 3, HEADS, HEAD_DIM)
    places = lax.axis_index("seq") * place_count + jnp.arange(place_count)

    def rope_piece(raw_values):
        return jnp.stack(
            [
                rotate(raw_values[:, :, 0], places),
                rotate(raw_values[:, :, 1], places),
                raw_values[:, :, 2],
            ],
            2,
        )

    rotated, rope_pull = jax.vjp(rope_piece, raw_qkv)
    outgoing = rotated.astype(jnp.bfloat16).reshape(row_count, place_count, 3, seq_size, -1)
    received = lax.all_to_all(outgoing, "seq", split_axis=3, concat_axis=1, tiled=True)
    full_length = received.shape[1]
    received = received.reshape(row_count, full_length, 3, -1, HEAD_DIM)
    mixed_heads, log_totals = lax.map(forward_row, (received, families))
    group_width = mixed_heads.shape[2] * HEAD_DIM
    returned = lax.all_to_all(
        mixed_heads.reshape(row_count, full_length, 1, group_width),
        "seq",
        split_axis=1,
        concat_axis=2,
        tiled=True,
    )
    heads_low = returned.reshape(token_count, model_width)
    attn_out = jnp.dot(heads_low, out_weight, preferred_element_type=jnp.float32)
    hidden = jnp.dot(normed_low, up_weight, preferred_element_type=jnp.float32) + up_bias
    active, gelu_pull = jax.vjp(gelu_piece, hidden)
    active_low = active.astype(jnp.bfloat16)
    mlp_out = jnp.dot(active_low, down_weight, preferred_element_type=jnp.float32) + down_bias
    layer_out = (
        (values.reshape(token_count, model_width) + attn_out + mlp_out)
        .astype(jnp.bfloat16)
        .reshape(inputs.shape)
    )
    local_rows = partners - lax.axis_index("dp") * row_count
    grad_low = jnp.take(cotangent, local_rows, axis=0).reshape(token_count, model_width)
    down_grad = jnp.einsum("tf,td->fd", active_low, grad_low, preferred_element_type=jnp.float32)
    down_bias_grad = jnp.sum(grad_low.astype(jnp.float32), 0)
    out_grad = jnp.einsum("te,td->ed", heads_low, grad_low, preferred_element_type=jnp.float32)
    d_active = jnp.einsum("td,fd->tf", grad_low, down_weight, preferred_element_type=jnp.float32)
    d_hidden_low = gelu_pull(d_active)[0].astype(jnp.bfloat16)
    up_bias_grad = jnp.sum(d_hidden_low.astype(jnp.float32), 0)
    up_grad = jnp.einsum("td,tf->df", normed_low, d_hidden_low, preferred_element_type=jnp.float32)
    d_heads = jnp.einsum(
        "td,ed->te", grad_low, out_weight, preferred_element_type=jnp.float32
    ).astype(jnp.bfloat16)
    d_heads = d_heads.reshape(row_count, place_count, seq_size, group_width)
    d_heads_split = lax.all_to_all(d_heads, "seq", split_axis=2, concat_axis=1, tiled=True)
    d_heads_split = d_heads_split.reshape(row_count, full_length, -1, HEAD_DIM)
    d_blocks = lax.map(backward_row, (received, families, log_totals, d_heads_split))
    d_blocks = d_blocks.reshape(row_count, full_length, 3, 1, group_width)
    d_rotated = lax.all_to_all(d_blocks, "seq", split_axis=1, concat_axis=3, tiled=True)
    d_rotated = d_rotated.reshape(row_count, place_count, 3, HEADS, HEAD_DIM).astype(jnp.float32)
    d_raw_low = rope_pull(d_rotated)[0].astype(jnp.bfloat16).reshape(token_count, 3 * model_width)
    qkv_grad = jnp.einsum("td,te->de", normed_low, d_raw_low, preferred_element_type=jnp.float32)
    d_normed = jnp.einsum("te,de->td", d_raw_low, qkv_weight, preferred_element_type=jnp.float32)
    d_normed = d_normed + jnp.einsum(
        "tf,df->td", d_hidden_low, up_weight, preferred_element_type=jnp.float32
    )
    d_values, gain_grad, shift_grad = norm_pull(d_normed.reshape(inputs.shape))
    input_grad = grad_low.astype(jnp.float32).reshape(inputs.shape) + d_values
    gain_sum, shift_sum, up_bias_sum, down_bias_sum = lax.psum(
        (gain_grad, shift_grad, up_bias_grad, down_bias_grad), ("dp", "seq")
    )
    partial_sums = (
        lax.psum_scatter(qkv_grad, "seq", scatter_dimension=1, tiled=True),
        lax.psum_scatter(out_grad, "seq", scatter_dimension=1, tiled=True),
        lax.psum_scatter(up_grad, "seq", scatter_dimension=1, tiled=True),
        lax.psum_scatter(down_grad, "seq", scatter_dimension=1, tiled=True),
    )
    qkv_sum, out_sum, up_sum, down_sum = (
        lax.psum_scatter(partial_sums[0], "dp", scatter_dimension=0, tiled=True),
        lax.psum_scatter(partial_sums[1], "dp", scatter_dimension=0, tiled=True),
        lax.psum_scatter(partial_sums[2], "dp", scatter_dimension=0, tiled=True),
        lax.psum_scatter(partial_sums[3], "dp", scatter_dimension=0, tiled=True),
    )
    return (
        layer_out,
        input_grad,
        gain_sum,
        shift_sum,
        qkv_sum,
        out_sum,
        up_sum,
        up_bias_sum,
        down_sum,
        down_bias_sum,
    )


def solution(mesh):
    placed = (
        P("dp", "seq", None),
        P(),
        P(),
        P(),
        P(),
        P(),
        P(),
        P(),
        P(),
        P("dp"),
        P("dp", None),
        P("dp", "seq", None),
    )
    return jax.shard_map(
        on_device,
        mesh=mesh,
        in_specs=placed,
        out_specs=(
            P("dp", "seq", None),
            P("dp", "seq", None),
            P(),
            P(),
            P("dp", "seq"),
            P("dp", "seq"),
            P("dp", "seq"),
            P(),
            P("dp", "seq"),
            P(),
        ),
        check_vma=False,
    )
```

profile of v0, /device:TPU:0, one launch (start us, length us, event | category | flops | bytes accessed | tf_op | source)
XLA Modules:
  0.0 1331.5 jit_solution(15439892296866444212)
XLA Ops:
  96.9 58.3 %all-to-all-done = bf16[4,256,3,4,256]{1,4,0,2,3:T(8,128)(2,1)} async-done(((bf16[4,256,3,4,256]{1,4,0,2,3:T(8,128)(2,1)}), bf16[4,256,3,4,256]{1,4,0,2,3:T(8,128)(2,1)}, u32[]{:S(2)}, u32[]{:S(2)}) %all-to-all-start) | async-done | bytes 6291488 | tf_op jit(solution)/shard_map/all_to_all | solution.py:124
  176.4 60.7 %while.22 = (s32[]{:T(128)}, bf16[4,1024,4,64]{1,3,2,0:T(8,128)(2,1)}, f32[4,4,1024]{2,1,0:T(4,128)}, bf16[4,1024,3,4,64]{1,4,3,2,0:T(8,128)(2,1)}, s32[4,1024]{1,0:T(4,128)S(1)}, /*index=5*/s32[]{:T(128)}) while((s32[]{:T(128)}, bf16[4,1024,4,64]{1,3,2,0:T(8,128)(2,1)}, f32[4,4,1024]{2,1,0:T(4,128)}, bf16[4,1024,3,4,64]{1,4,3,2,0:T(8,128)(2,1)}, ...), condition=%wide.region_5.6_spmd, body=%wide.region_2.5_spmd.sunk | while | flops 1127477248 | bytes 59913292 | solution.py:127
  246.0 208.5 %while.23 = (s32[]{:T(128)}, bf16[4,1024,3,4,64]{1,4,3,2,0:T(8,128)(2,1)}, bf16[4,1024,3,4,64]{1,4,3,2,0:T(8,128)(2,1)}, s32[4,1024]{1,0:T(4,128)S(1)}, f32[4,4,...) while((s32[]{:T(128)}, bf16[4,1024,3,4,64]{1,4,3,2,0:T(8,128)(2,1)}, ...), condition=%wide.region_8.9_spmd, body=%wide.region_6.8_spmd.sunk | while | flops 2731274240 | bytes 196179696 | solution.py:162
  258.5 12.7 multiply_reduce_fusion.5
  310.6 12.7 multiply_reduce_fusion.5
  323.3 11.9 multiply_convert_fusion.5
  362.7 12.7 multiply_reduce_fusion.5
  375.4 11.9 multiply_convert_fusion.5
  414.8 12.7 multiply_reduce_fusion.5
  480.8 82.8 %all-to-all-done.3 = bf16[4,1024,3,1,256]{4,0,3,2,1:T(4,128)(2,1)} async-done(((bf16[4,1024,3,1,256]{4,0,3,2,1:T(4,128)(2,1)}), bf16[4,1024,3,1,256]{4,0,3,2,1:T(4,128)(2,1)}, u32[]{:S(2)}, u32[]{:S(2)}) %all-to-all-start.3) | async-done | bytes 6291488 | tf_op jit(solution)/shard_map/all_to_all | solution.py:164
  573.6 12.6 copy.120
  638.2 18.6 %fusion.48 = f32[1024,4096]{1,0:T(8,128)} fusion(bf16[1024,1024]{1,0:T(8,128)(2,1)} %bitcast.215, bf16[1024,4096]{1,0:T(8,128)(2,1)} %param.21), kind=kOutput, calls=%fused_computation.117 | convolution fusion | flops 8589934592 | bytes 27262976 | tf_op jit(solution)/shard_map/dot_general | solution.py:138
  656.8 26.5 %convert_reduce_fusion = (f32[4096]{0:T(1024)S(1)}, bf16[1024,4096]{1,0:T(8,128)(2,1)}) fusion(f32[1024,4096]{1,0:T(8,128)} %fusion.48, f32[4096]{0:T(1024)S(1)} %copy-done.28, bf16[1024,1024]{1,0:T(8,128)(2,1)} %copy-done.9, bf16[4096,1024]{1,0:T(8,128)(2,1)} %param.23), kind=kOutput, calls=%fused_computation.59 | convolution fusion | flops 8686399488 | bytes 35684352 | tf_op jit(solution)/shard_map/td,fd->tf/dot_general | solution.py:152
  683.3 16.3 %fusion.52 = f32[1024,4096]{1,0:T(8,128)} fusion(bf16[1024,1024]{1,0:T(8,128)(2,1)} %bitcast.216, bf16[1024,4096]{1,0:T(8,128)(2,1)} %get-tuple-element.104), kind=kOutput, calls=%fused_computation.121 | convolution fusion | flops 8589934592 | bytes 27262976 | tf_op jit(solution)/shard_map/td,tf->df/dot_general | solution.py:155
  699.7 20.1 %fusion.43 = f32[4096,1024]{1,0:T(8,128)} fusion(bf16[1024,1024]{1,0:T(8,128)(2,1)} %copy-done.9, f32[1024,4096]{1,0:T(8,128)} %fusion.48, f32[4096]{0:T(1024)S(1)} %copy-done.28), kind=kOutput, calls=%fused_computation.113 | convolution fusion | flops 8631877632 | bytes 35667968 | tf_op jit(solution)/shard_map/tf,td->fd/dot_general | solution.py:149
  720.5 17.9 %reduce-scatter.9.cloned.1.call-done = f32[1024,768]{1,0:T(8,128)} async-done(((f32[1024,3072]{1,0:T(8,128)}), f32[1024,768]{1,0:T(8,128)}) %reduce-scatter.9.cloned.1.call-update) | async-done | bytes 3145744 | tf_op jit(solution)/shard_map/reduce_scatter | solution.py:178
  738.5 128.8 %reduce-scatter.17.cloned.1.call-done = f32[1024,1024]{1,0:T(8,128)} async-done(((f32[1024,4096]{1,0:T(8,128)}), f32[1024,1024]{1,0:T(8,128)}) %reduce-scatter.17.cloned.1.call-update) | async-done | bytes 4194320 | tf_op jit(solution)/shard_map/reduce_scatter | solution.py:180
  873.3 122.5 %reduce-scatter.21.cloned.1.call-done = f32[4096,256]{1,0:T(8,128)} async-done(((f32[4096,1024]{1,0:T(8,128)}), f32[4096,256]{1,0:T(8,128)}) %reduce-scatter.21.cloned.1.call-update) | async-done | bytes 4194320 | tf_op jit(solution)/shard_map/reduce_scatter | solution.py:181
  995.9 19.7 %fusion.38 = bf16[1024,1024]{1,0:T(8,128)(2,1)} fusion(f32[1024,1024]{1,0:T(8,128)} %fusion.47, bf16[4,256,1024]{2,1,0:T(8,128)(2,1)} %param.16, f32[1024]{0:T(1024)S(1)} %copy-done.29, bf16[4096,1024]{1,0:T(8,128)(2,1)} %param.23, f32[1024,4096]{1,0:T(8,128)} %fusion.48, f32[4096]{0:T(1024)S(1)} %copy-done.28), kind=kOutput, calls=%fused_computation.74 | convolution fusion | flops 8637120512 | bytes 33574912 | tf_op jit(solution)/shard_map/dot_general | solution.py:141
  1026.3 14.2 %fusion.46 = (f32[1024]{0:T(1024)S(1)}, f32[1024,1024]{1,0:T(8,128)S(1)}) fusion(f32[1024,1024]{1,0:T(8,128)S(1)} %fusion.49, bf16[1024,4096]{1,0:T(8,128)(2,1)} %get-tuple-element.104, bf16[1024,4096]{1,0:T(8,128)(2,1)} %param.21), kind=kOutput, calls=%fused_computation.115 | convolution fusion | flops 8592030720 | bytes 25169920 | tf_op jit(solution)/shard_map/tf,df->td/dot_general | solution.py:169
  1043.5 40.4 %all-reduce.9 = (f32[1024]{0:T(1024)}, f32[1024]{0:T(1024)}, f32[4096]{0:T(1024)}, f32[1024]{0:T(1024)}) all-reduce(f32[1024]{0:T(1024)S(1)} %get-tuple-element.73, f32[1024]{0:T(1024)S(1)} %get-tuple-element.130, f32[4096]{0:T(1024)S(1)} %get-tuple-element.103, f32[1024]{0:T(1024)S(1)} %copy-done.26), channel_id=1, replica_groups=mesh['dp'=8,'seq'=4] {'dp','seq'}, use_global_device_ids=true, to_apply=%region_12.13 | all-reduce | flops 7168 | bytes 57344 | tf_op jit(solution)/shard_map/psum | solution.py:174
  1089.6 51.3 %reduce-scatter.11.cloned.1.call-done = f32[128,768]{1,0:T(8,128)} async-done(((f32[1024,768]{1,0:T(8,128)}), f32[128,768]{1,0:T(8,128)}) %reduce-scatter.11.cloned.1.call-update) | async-done | bytes 393232 | tf_op jit(solution)/shard_map/reduce_scatter | solution.py:184
  1140.9 91.2 %reduce-scatter.19.cloned.1.call-done = f32[128,1024]{1,0:T(8,128)} async-done(((f32[1024,1024]{1,0:T(8,128)}), f32[128,1024]{1,0:T(8,128)}) %reduce-scatter.19.cloned.1.call-update) | async-done | bytes 524304 | tf_op jit(solution)/shard_map/reduce_scatter | solution.py:186
  1232.1 92.3 %reduce-scatter.23.cloned.1.call-done = f32[512,256]{1,0:T(8,128)} async-done(((f32[4096,256]{1,0:T(8,128)}), f32[512,256]{1,0:T(8,128)}) %reduce-scatter.23.cloned.1.call-update) | async-done | bytes 524304 | tf_op jit(solution)/shard_map/reduce_scatter | solution.py:187
  (252 shorter events, 428.0 us)
Async XLA Ops:
  26.4 51.6 %all-to-all-start.2 = ((bf16[4,256,4,256]{3,1,0,2:T(8,128)(2,1)}), bf16[4,256,4,256]{3,1,0,2:T(8,128)(2,1)}, u32[]{:S(2)}, u32[]{:S(2)}) async-start(bf16[4,256,4,256]{3,1,0,2:T(8,128)(2,1)} %copy.116), calls=%async_computation.2 | async-start | bytes 4194304 | tf_op jit(solution)/shard_map/all_to_all | solution.py:160
  78.0 77.2 %all-to-all-start = ((bf16[4,256,3,4,256]{1,4,0,2,3:T(8,128)(2,1)}), bf16[4,256,3,4,256]{1,4,0,2,3:T(8,128)(2,1)}, u32[]{:S(2)}, u32[]{:S(2)}) async-start(bf16[4,256,3,4,256]{1,4,0,2,3:T(8,128)(2,1)} %copy.127), calls=%async_computation | async-start | bytes 12582912 | tf_op jit(solution)/shard_map/all_to_all | solution.py:124
  241.4 223.9 %all-to-all-start.1 = ((bf16[4,1024,1,256]{3,0,2,1:T(4,128)(2,1)}), bf16[4,1024,1,256]{3,0,2,1:T(4,128)(2,1)}, u32[]{:S(2)}, u32[]{:S(2)}) async-start(bf16[4,1024,1,256]{3,0,2,1:T(4,128)(2,1)} %copy.113), calls=%async_computation.1 | async-start | bytes 4194304 | tf_op jit(solution)/shard_map/all_to_all | solution.py:129
  271.2 20.0 %slice-start = ((s8[16777216]{0:T(1024)(128)(4,1)}), s8[4194304]{0:T(1024)(128)(4,1)S(1)}, s32[]{:S(2)}) async-start(s8[16777216]{0:T(1024)(128)(4,1)} %bitcast.198), calls=%async_computation.20 | async-start | bytes 8388608 | tf_op jit(solution)/shard_map/while
  271.2 20.0 %slice-start.1 = ((s8[16777216]{0:T(1024)(128)(4,1)}), s8[4194304]{0:T(1024)(128)(4,1)S(1)}, s32[]{:S(2)}) async-start(s8[16777216]{0:T(1024)(128)(4,1)} %bitcast.198), calls=%async_computation.21 | async-start | bytes 8388608 | tf_op jit(solution)/shard_map/while
  271.2 20.0 %slice-start.2 = ((s8[16777216]{0:T(1024)(128)(4,1)}), s8[4194304]{0:T(1024)(128)(4,1)S(1)}, s32[]{:S(2)}) async-start(s8[16777216]{0:T(1024)(128)(4,1)} %bitcast.198), calls=%async_computation.22 | async-start | bytes 8388608 | tf_op jit(solution)/shard_map/while
  323.2 20.0 %slice-start = ((s8[16777216]{0:T(1024)(128)(4,1)}), s8[4194304]{0:T(1024)(128)(4,1)S(1)}, s32[]{:S(2)}) async-start(s8[16777216]{0:T(1024)(128)(4,1)} %bitcast.198), calls=%async_computation.20 | async-start | bytes 8388608 | tf_op jit(solution)/shard_map/while
  323.3 20.0 %slice-start.1 = ((s8[16777216]{0:T(1024)(128)(4,1)}), s8[4194304]{0:T(1024)(128)(4,1)S(1)}, s32[]{:S(2)}) async-start(s8[16777216]{0:T(1024)(128)(4,1)} %bitcast.198), calls=%async_computation.21 | async-start | bytes 8388608 | tf_op jit(solution)/shard_map/while
  323.3 20.0 %slice-start.2 = ((s8[16777216]{0:T(1024)(128)(4,1)}), s8[4194304]{0:T(1024)(128)(4,1)S(1)}, s32[]{:S(2)}) async-start(s8[16777216]{0:T(1024)(128)(4,1)} %bitcast.198), calls=%async_computation.22 | async-start | bytes 8388608 | tf_op jit(solution)/shard_map/while
  375.4 20.0 %slice-start = ((s8[16777216]{0:T(1024)(128)(4,1)}), s8[4194304]{0:T(1024)(128)(4,1)S(1)}, s32[]{:S(2)}) async-start(s8[16777216]{0:T(1024)(128)(4,1)} %bitcast.198), calls=%async_computation.20 | async-start | bytes 8388608 | tf_op jit(solution)/shard_map/while
  375.4 20.0 %slice-start.1 = ((s8[16777216]{0:T(1024)(128)(4,1)}), s8[4194304]{0:T(1024)(128)(4,1)S(1)}, s32[]{:S(2)}) async-start(s8[16777216]{0:T(1024)(128)(4,1)} %bitcast.198), calls=%async_computation.21 | async-start | bytes 8388608 | tf_op jit(solution)/shard_map/while
  375.4 20.0 %slice-start.2 = ((s8[16777216]{0:T(1024)(128)(4,1)}), s8[4194304]{0:T(1024)(128)(4,1)S(1)}, s32[]{:S(2)}) async-start(s8[16777216]{0:T(1024)(128)(4,1)} %bitcast.198), calls=%async_computation.22 | async-start | bytes 8388608 | tf_op jit(solution)/shard_map/while
  427.5 20.0 %slice-start = ((s8[16777216]{0:T(1024)(128)(4,1)}), s8[4194304]{0:T(1024)(128)(4,1)S(1)}, s32[]{:S(2)}) async-start(s8[16777216]{0:T(1024)(128)(4,1)} %bitcast.198), calls=%async_computation.20 | async-start | bytes 8388608 | tf_op jit(solution)/shard_map/while
  427.5 20.0 %slice-start.1 = ((s8[16777216]{0:T(1024)(128)(4,1)}), s8[4194304]{0:T(1024)(128)(4,1)S(1)}, s32[]{:S(2)}) async-start(s8[16777216]{0:T(1024)(128)(4,1)} %bitcast.198), calls=%async_computation.21 | async-start | bytes 8388608 | tf_op jit(solution)/shard_map/while
  465.2 98.4 %all-to-all-start.3 = ((bf16[4,1024,3,1,256]{4,0,3,2,1:T(4,128)(2,1)}), bf16[4,1024,3,1,256]{4,0,3,2,1:T(4,128)(2,1)}, u32[]{:S(2)}, u32[]{:S(2)}) async-start(bf16[4,1024,3,1,256]{4,0,3,2,1:T(4,128)(2,1)} %copy.118), calls=%async_computation.3 | async-start | bytes 12582912 | tf_op jit(solution)/shard_map/all_to_all | solution.py:164
  470.5 249.4 %reduce-scatter.13.cloned.1.call-start = ((), (), s32[]{:S(2)}) async-start(), calls=%async_computation.14 | async-start | bytes 5242880 | tf_op jit(solution)/shard_map/reduce_scatter | solution.py:179
  480.8 257.6 %reduce-scatter.9.cloned.1.call-start = ((), (), s32[]{:S(2)}) async-start(), calls=%async_computation.12 | async-start | bytes 15728640 | tf_op jit(solution)/shard_map/reduce_scatter | solution.py:178
  638.1 229.2 %reduce-scatter.17.cloned.1.call-start = ((), (), s32[]{:S(2)}) async-start(), calls=%async_computation.16 | async-start | bytes 20971520 | tf_op jit(solution)/shard_map/reduce_scatter | solution.py:180
  699.7 296.2 %reduce-scatter.21.cloned.1.call-start = ((), (), s32[]{:S(2)}) async-start(), calls=%async_computation.18 | async-start | bytes 20971520 | tf_op jit(solution)/shard_map/reduce_scatter | solution.py:181
  719.8 369.7 %reduce-scatter.15.cloned.1.call-start = ((), (), s32[]{:S(2)}) async-start(), calls=%async_computation.15 | async-start | bytes 1179648 | tf_op jit(solution)/shard_map/reduce_scatter | solution.py:185
  720.4 420.5 %reduce-scatter.11.cloned.1.call-start = ((), (), s32[]{:S(2)}) async-start(), calls=%async_computation.13 | async-start | bytes 3538944 | tf_op jit(solution)/shard_map/reduce_scatter | solution.py:184
  738.4 493.7 %reduce-scatter.19.cloned.1.call-start = ((), (), s32[]{:S(2)}) async-start(), calls=%async_computation.17 | async-start | bytes 4718592 | tf_op jit(solution)/shard_map/reduce_scatter | solution.py:186
  867.3 457.1 %reduce-scatter.23.cloned.1.call-start = ((), (), s32[]{:S(2)}) async-start(), calls=%async_computation.19 | async-start | bytes 4718592 | tf_op jit(solution)/shard_map/reduce_scatter | solution.py:187
  873.3 122.6 %copy-start.29 = (f32[1024]{0:T(1024)S(1)}, f32[1024]{0:T(1024)}, u32[]{:S(2)}) copy-start(f32[1024]{0:T(1024)} %param.24) | copy-start | bytes 12292
  (37 other events, 258.2 us)
Sparse Core Ops, SparseCore 0:
  480.9 69.5 reduce-scatter.12
  638.2 100.1 reduce-scatter.8
  741.1 126.0 reduce-scatter.16
  869.7 126.0 reduce-scatter.20
  1000.0 63.4 reduce-scatter.14
  1067.6 73.3 reduce-scatter.10
  1145.1 86.9 reduce-scatter.18
  1236.7 87.6 reduce-scatter.22
where the time goes:
time: 1340 us; the launch traced here: 1330 us
  waiting for transfers between devices  646 us (48%)
  matrix products  334 us (25%)
  local copies, waits for them, and re-layouts  152 us (11%)
  other arithmetic  123 us (9%)
  blocking collectives  40.4 us (3%)
  starting transfers between devices  21.1 us (2%)
  between operations  14.8 us (1%)
    reduce_scatter x1, waiting for transfers between devices, on_device(): lax.psum_scatter(up_grad, 'seq', scatter_dimension=1, tiled=True)  129 us
    reduce_scatter x1, waiting for transfers between devices, on_device(): lax.psum_scatter(down_grad, 'seq', scatter_dimension=1, tiled=True)  123 us
    reduce_scatter x1, waiting for transfers between devices, on_device(): lax.psum_scatter(partial_sums[3], 'dp', scatter_dimension=0, tiled=True)  92.3 us
    reduce_scatter x1, waiting for transfers between devices, on_device(): lax.psum_scatter(partial_sums[2], 'dp', scatter_dimension=0, tiled=True)  91.2 us
    all_to_all x1, waiting for transfers between devices, on_device(): lax.all_to_all(d_blocks, 'seq', split_axis=1, concat_axis=3, tiled=True)  82.8 us
    dot_general x8, matrix products, masked_scores(): jnp.einsum('qhd,khd->hqk', queries, key_rows, preferred_element_type=jnp....  62.9 us
    all_to_all x1, waiting for transfers between devices, on_device(): lax.all_to_all(outgoing, 'seq', split_axis=3, concat_axis=1, tiled=True)  58.3 us
    reduce_scatter x1, waiting for transfers between devices, on_device(): lax.psum_scatter(partial_sums[0], 'dp', scatter_dimension=0, tiled=True)  51.3 us
  transfers between devices with their start and end apart: 12, of which 8 were waited for; matrix products, arithmetic and copies ran while one was open for 37% of the time, Pallas kernels for 0%

commit v1 on v0

--- a/solution.py
+++ b/solution.py
@@ -7,6 +7,12 @@
 HEAD_DIM = 64
 ROT = 32
 EPS = 1e-05
+
+
+def swap_blocks(x, axis, split, join):
+    pieces = jnp.split(x, lax.axis_size(axis), axis=split)
+    received = lax.all_to_all(jnp.stack(pieces), axis, 0, 0)
+    return jnp.concatenate(received, axis=join)
 
 
 def norm_piece(values, norm_gain, norm_shift):
@@ -121,7 +127,7 @@
 
     rotated, rope_pull = jax.vjp(rope_piece, raw_qkv)
     outgoing = rotated.astype(jnp.bfloat16).reshape(row_count, place_count, 3, seq_size, -1)
-    received = lax.all_to_all(outgoing, "seq", split_axis=3, concat_axis=1, tiled=True)
+    received = swap_blocks(outgoing, "seq", 3, 1)
     full_length = received.shape[1]
     received = received.reshape(row_count, full_length, 3, -1, HEAD_DIM)
     mixed_heads, log_totals = lax.map(forward_row, (received, families))

time: 1340 us -> 1340 us (level)
  no operation moved by 1% of the time
where the time goes in v1:
time: 1340 us; the launch traced here: 1330 us
  waiting for transfers between devices  646 us (48%)
  matrix products  334 us (25%)
  local copies, waits for them, and re-layouts  148 us (11%)
  other arithmetic  125 us (9%)
  blocking collectives  40.4 us (3%)
  starting transfers between devices  21.1 us (2%)
  between operations  14.9 us (1%)
    reduce_scatter x1, waiting for transfers between devices, on_device(): lax.psum_scatter(up_grad, 'seq', scatter_dimension=1, tiled=True)  129 us
    reduce_scatter x1, waiting for transfers between devices, on_device(): lax.psum_scatter(down_grad, 'seq', scatter_dimension=1, tiled=True)  123 us
    reduce_scatter x1, waiting for transfers between devices, on_device(): lax.psum_scatter(partial_sums[3], 'dp', scatter_dimension=0, tiled=True)  92.5 us
    reduce_scatter x1, waiting for transfers between devices, on_device(): lax.psum_scatter(partial_sums[2], 'dp', scatter_dimension=0, tiled=True)  91.5 us
    all_to_all x1, waiting for transfers between devices, on_device(): lax.all_to_all(d_blocks, 'seq', split_axis=1, concat_axis=3, tiled=True)  82.8 us
    dot_general x8, matrix products, masked_scores(): jnp.einsum('qhd,khd->hqk', queries, key_rows, preferred_element_type=jnp....  62.8 us
    all_to_all x1, waiting for transfers between devices, swap_blocks(): received = lax.all_to_all(jnp.stack(pieces), axis, 0, 0)  58.3 us
    reduce_scatter x1, waiting for transfers between devices, on_device(): lax.psum_scatter(partial_sums[0], 'dp', scatter_dimension=0, tiled=True)  51.1 us
  transfers between devices with their start and end apart: 12, of which 8 were waited for; matrix products, arithmetic and copies ran while one was open for 37% of the time, Pallas kernels for 0%

profile of v1, /device:TPU:0, one launch (start us, length us, event | category | flops | bytes accessed | tf_op | source)
XLA Modules:
  0.0 1330.8 jit_solution(2190498893878276495)
XLA Ops:
  96.1 58.3 %all-to-all-done = bf16[4,4,256,3,1,256]{2,5,1,3,4,0:T(8,128)(2,1)} async-done(((bf16[4,4,256,3,1,256]{2,5,1,3,4,0:T(8,128)(2,1)}), bf16[4,4,256,3,1,256]{2,5,1,3,4,0:T(8,128)(2,1)}, u32[]{:S(2)}, u32[]{:S(2)}) %all-to-all-start) | async-done | bytes 6291488 | tf_op jit(solution)/shard_map/all_to_all | solution.py:14
  175.7 60.7 %while.22 = (s32[]{:T(128)}, bf16[4,1024,4,64]{1,3,2,0:T(8,128)(2,1)}, f32[4,4,1024]{2,1,0:T(4,128)}, bf16[4,1024,3,4,64]{1,4,3,2,0:T(8,128)(2,1)}, s32[4,1024]{1,0:T(4,128)S(1)}, /*index=5*/s32[]{:T(128)}) while((s32[]{:T(128)}, bf16[4,1024,4,64]{1,3,2,0:T(8,128)(2,1)}, f32[4,4,1024]{2,1,0:T(4,128)}, bf16[4,1024,3,4,64]{1,4,3,2,0:T(8,128)(2,1)}, ...), condition=%wide.region_5.6_spmd, body=%wide.region_2.5_spmd.sunk | while | flops 1127477248 | bytes 59913292 | solution.py:133
  245.3 208.4 %while.23 = (s32[]{:T(128)}, bf16[4,1024,3,4,64]{1,4,3,2,0:T(8,128)(2,1)}, bf16[4,1024,3,4,64]{1,4,3,2,0:T(8,128)(2,1)}, s32[4,1024]{1,0:T(4,128)S(1)}, f32[4,4,...) while((s32[]{:T(128)}, bf16[4,1024,3,4,64]{1,4,3,2,0:T(8,128)(2,1)}, ...), condition=%wide.region_8.9_spmd, body=%wide.region_6.8_spmd.sunk | while | flops 2731274240 | bytes 196179696 | solution.py:168
  257.7 12.7 multiply_reduce_fusion.5
  270.4 11.9 multiply_convert_fusion.5
  309.8 12.7 multiply_reduce_fusion.5
  322.5 11.9 multiply_convert_fusion.5
  361.9 12.7 multiply_reduce_fusion.5
  414.0 12.7 multiply_reduce_fusion.5
  480.1 82.8 %all-to-all-done.3 = bf16[4,1024,3,1,256]{4,0,3,2,1:T(4,128)(2,1)} async-done(((bf16[4,1024,3,1,256]{4,0,3,2,1:T(4,128)(2,1)}), bf16[4,1024,3,1,256]{4,0,3,2,1:T(4,128)(2,1)}, u32[]{:S(2)}, u32[]{:S(2)}) %all-to-all-start.3) | async-done | bytes 6291488 | tf_op jit(solution)/shard_map/all_to_all | solution.py:170
  572.8 12.6 copy.133
  637.2 18.6 %fusion.48 = f32[1024,4096]{1,0:T(8,128)} fusion(bf16[1024,1024]{1,0:T(8,128)(2,1)} %bitcast.227, bf16[1024,4096]{1,0:T(8,128)(2,1)} %param.21), kind=kOutput, calls=%fused_computation.122 | convolution fusion | flops 8589934592 | bytes 27262976 | tf_op jit(solution)/shard_map/dot_general | solution.py:144
  655.9 26.3 %convert_reduce_fusion = (f32[4096]{0:T(1024)S(1)}, bf16[1024,4096]{1,0:T(8,128)(2,1)}) fusion(f32[1024,4096]{1,0:T(8,128)} %fusion.48, f32[4096]{0:T(1024)S(1)} %copy-done.28, bf16[1024,1024]{1,0:T(8,128)(2,1)} %copy-done.9, bf16[4096,1024]{1,0:T(8,128)(2,1)} %param.23), kind=kOutput, calls=%fused_computation.59 | convolution fusion | flops 8686399488 | bytes 35684352 | tf_op jit(solution)/shard_map/td,fd->tf/dot_general | solution.py:158
  682.2 16.3 %fusion.52 = f32[1024,4096]{1,0:T(8,128)} fusion(bf16[1024,1024]{1,0:T(8,128)(2,1)} %bitcast.228, bf16[1024,4096]{1,0:T(8,128)(2,1)} %get-tuple-element.104), kind=kOutput, calls=%fused_computation.126 | convolution fusion | flops 8589934592 | bytes 27262976 | tf_op jit(solution)/shard_map/td,tf->df/dot_general | solution.py:161
  698.6 20.1 %fusion.43 = f32[4096,1024]{1,0:T(8,128)} fusion(bf16[1024,1024]{1,0:T(8,128)(2,1)} %copy-done.9, f32[1024,4096]{1,0:T(8,128)} %fusion.48, f32[4096]{0:T(1024)S(1)} %copy-done.28), kind=kOutput, calls=%fused_computation.118 | convolution fusion | flops 8631877632 | bytes 35667968 | tf_op jit(solution)/shard_map/tf,td->fd/dot_general | solution.py:155
  719.4 18.1 %reduce-scatter.9.cloned.1.call-done = f32[1024,768]{1,0:T(8,128)} async-done(((f32[1024,3072]{1,0:T(8,128)}), f32[1024,768]{1,0:T(8,128)}) %reduce-scatter.9.cloned.1.call-update) | async-done | bytes 3145744 | tf_op jit(solution)/shard_map/reduce_scatter | solution.py:184
  737.5 128.8 %reduce-scatter.17.cloned.1.call-done = f32[1024,1024]{1,0:T(8,128)} async-done(((f32[1024,4096]{1,0:T(8,128)}), f32[1024,1024]{1,0:T(8,128)}) %reduce-scatter.17.cloned.1.call-update) | async-done | bytes 4194320 | tf_op jit(solution)/shard_map/reduce_scatter | solution.py:186
  872.4 122.6 %reduce-scatter.21.cloned.1.call-done = f32[4096,256]{1,0:T(8,128)} async-done(((f32[4096,1024]{1,0:T(8,128)}), f32[4096,256]{1,0:T(8,128)}) %reduce-scatter.21.cloned.1.call-update) | async-done | bytes 4194320 | tf_op jit(solution)/shard_map/reduce_scatter | solution.py:187
  995.0 19.7 %fusion.38 = bf16[1024,1024]{1,0:T(8,128)(2,1)} fusion(f32[1024,1024]{1,0:T(8,128)} %fusion.47, bf16[4,256,1024]{2,1,0:T(8,128)(2,1)} %param.16, f32[1024]{0:T(1024)S(1)} %copy-done.29, bf16[4096,1024]{1,0:T(8,128)(2,1)} %param.23, f32[1024,4096]{1,0:T(8,128)} %fusion.48, f32[4096]{0:T(1024)S(1)} %copy-done.28), kind=kOutput, calls=%fused_computation.75 | convolution fusion | flops 8637120512 | bytes 33574912 | tf_op jit(solution)/shard_map/dot_general | solution.py:147
  1025.4 14.2 %fusion.46 = (f32[1024]{0:T(1024)S(1)}, f32[1024,1024]{1,0:T(8,128)S(1)}) fusion(f32[1024,1024]{1,0:T(8,128)S(1)} %fusion.49, bf16[1024,4096]{1,0:T(8,128)(2,1)} %get-tuple-element.104, bf16[1024,4096]{1,0:T(8,128)(2,1)} %param.21), kind=kOutput, calls=%fused_computation.120 | convolution fusion | flops 8592030720 | bytes 25169920 | tf_op jit(solution)/shard_map/tf,df->td/dot_general | solution.py:175
  1042.6 40.4 %all-reduce.9 = (f32[1024]{0:T(1024)}, f32[1024]{0:T(1024)}, f32[4096]{0:T(1024)}, f32[1024]{0:T(1024)}) all-reduce(f32[1024]{0:T(1024)S(1)} %get-tuple-element.73, f32[1024]{0:T(1024)S(1)} %get-tuple-element.134, f32[4096]{0:T(1024)S(1)} %get-tuple-element.103, f32[1024]{0:T(1024)S(1)} %copy-done.26), channel_id=1, replica_groups=mesh['dp'=8,'seq'=4] {'dp','seq'}, use_global_device_ids=true, to_apply=%region_12.13 | all-reduce | flops 7168 | bytes 57344 | tf_op jit(solution)/shard_map/psum | solution.py:180
  1088.7 51.1 %reduce-scatter.11.cloned.1.call-done = f32[128,768]{1,0:T(8,128)} async-done(((f32[1024,768]{1,0:T(8,128)}), f32[128,768]{1,0:T(8,128)}) %reduce-scatter.11.cloned.1.call-update) | async-done | bytes 393232 | tf_op jit(solution)/shard_map/reduce_scatter | solution.py:190
  1139.8 91.5 %reduce-scatter.19.cloned.1.call-done = f32[128,1024]{1,0:T(8,128)} async-done(((f32[1024,1024]{1,0:T(8,128)}), f32[128,1024]{1,0:T(8,128)}) %reduce-scatter.19.cloned.1.call-update) | async-done | bytes 524304 | tf_op jit(solution)/shard_map/reduce_scatter | solution.py:192
  1231.3 92.5 %reduce-scatter.23.cloned.1.call-done = f32[512,256]{1,0:T(8,128)} async-done(((f32[4096,256]{1,0:T(8,128)}), f32[512,256]{1,0:T(8,128)}) %reduce-scatter.23.cloned.1.call-update) | async-done | bytes 524304 | tf_op jit(solution)/shard_map/reduce_scatter | solution.py:193
  (253 shorter events, 427.1 us)
Async XLA Ops:
  26.4 50.9 %all-to-all-start.2 = ((bf16[4,256,4,256]{3,1,0,2:T(8,128)(2,1)}), bf16[4,256,4,256]{3,1,0,2:T(8,128)(2,1)}, u32[]{:S(2)}, u32[]{:S(2)}) async-start(bf16[4,256,4,256]{3,1,0,2:T(8,128)(2,1)} %copy.129), calls=%async_computation.2 | async-start | bytes 4194304 | tf_op jit(solution)/shard_map/all_to_all | solution.py:166
  77.3 77.2 %all-to-all-start = ((bf16[4,4,256,3,1,256]{2,5,1,3,4,0:T(8,128)(2,1)}), bf16[4,4,256,3,1,256]{2,5,1,3,4,0:T(8,128)(2,1)}, u32[]{:S(2)}, u32[]{:S(2)}) async-start(bf16[4,4,256,3,1,256]{2,5,1,3,4,0:T(8,128)(2,1)} %pad_maximum_fusion.1), calls=%async_computation | async-start | bytes 12582912 | tf_op jit(solution)/shard_map/all_to_all | solution.py:14
  240.6 223.8 %all-to-all-start.1 = ((bf16[4,1024,1,256]{3,0,2,1:T(4,128)(2,1)}), bf16[4,1024,1,256]{3,0,2,1:T(4,128)(2,1)}, u32[]{:S(2)}, u32[]{:S(2)}) async-start(bf16[4,1024,1,256]{3,0,2,1:T(4,128)(2,1)} %copy.126), calls=%async_computation.1 | async-start | bytes 4194304 | tf_op jit(solution)/shard_map/all_to_all | solution.py:135
  270.4 20.0 %slice-start = ((s8[16777216]{0:T(1024)(128)(4,1)}), s8[4194304]{0:T(1024)(128)(4,1)S(1)}, s32[]{:S(2)}) async-start(s8[16777216]{0:T(1024)(128)(4,1)} %bitcast.210), calls=%async_computation.20 | async-start | bytes 8388608 | tf_op jit(solution)/shard_map/while
  270.4 20.0 %slice-start.1 = ((s8[16777216]{0:T(1024)(128)(4,1)}), s8[4194304]{0:T(1024)(128)(4,1)S(1)}, s32[]{:S(2)}) async-start(s8[16777216]{0:T(1024)(128)(4,1)} %bitcast.210), calls=%async_computation.21 | async-start | bytes 8388608 | tf_op jit(solution)/shard_map/while
  270.4 20.0 %slice-start.2 = ((s8[16777216]{0:T(1024)(128)(4,1)}), s8[4194304]{0:T(1024)(128)(4,1)S(1)}, s32[]{:S(2)}) async-start(s8[16777216]{0:T(1024)(128)(4,1)} %bitcast.210), calls=%async_computation.22 | async-start | bytes 8388608 | tf_op jit(solution)/shard_map/while
  322.5 20.0 %slice-start = ((s8[16777216]{0:T(1024)(128)(4,1)}), s8[4194304]{0:T(1024)(128)(4,1)S(1)}, s32[]{:S(2)}) async-start(s8[16777216]{0:T(1024)(128)(4,1)} %bitcast.210), calls=%async_computation.20 | async-start | bytes 8388608 | tf_op jit(solution)/shard_map/while
  322.5 20.0 %slice-start.1 = ((s8[16777216]{0:T(1024)(128)(4,1)}), s8[4194304]{0:T(1024)(128)(4,1)S(1)}, s32[]{:S(2)}) async-start(s8[16777216]{0:T(1024)(128)(4,1)} %bitcast.210), calls=%async_computation.21 | async-start | bytes 8388608 | tf_op jit(solution)/shard_map/while
  322.5 20.0 %slice-start.2 = ((s8[16777216]{0:T(1024)(128)(4,1)}), s8[4194304]{0:T(1024)(128)(4,1)S(1)}, s32[]{:S(2)}) async-start(s8[16777216]{0:T(1024)(128)(4,1)} %bitcast.210), calls=%async_computation.22 | async-start | bytes 8388608 | tf_op jit(solution)/shard_map/while
  374.6 20.0 %slice-start = ((s8[16777216]{0:T(1024)(128)(4,1)}), s8[4194304]{0:T(1024)(128)(4,1)S(1)}, s32[]{:S(2)}) async-start(s8[16777216]{0:T(1024)(128)(4,1)} %bitcast.210), calls=%async_computation.20 | async-start | bytes 8388608 | tf_op jit(solution)/shard_map/while
  374.6 20.0 %slice-start.1 = ((s8[16777216]{0:T(1024)(128)(4,1)}), s8[4194304]{0:T(1024)(128)(4,1)S(1)}, s32[]{:S(2)}) async-start(s8[16777216]{0:T(1024)(128)(4,1)} %bitcast.210), calls=%async_computation.21 | async-start | bytes 8388608 | tf_op jit(solution)/shard_map/while
  374.6 20.0 %slice-start.2 = ((s8[16777216]{0:T(1024)(128)(4,1)}), s8[4194304]{0:T(1024)(128)(4,1)S(1)}, s32[]{:S(2)}) async-start(s8[16777216]{0:T(1024)(128)(4,1)} %bitcast.210), calls=%async_computation.22 | async-start | bytes 8388608 | tf_op jit(solution)/shard_map/while
  426.7 20.0 %slice-start = ((s8[16777216]{0:T(1024)(128)(4,1)}), s8[4194304]{0:T(1024)(128)(4,1)S(1)}, s32[]{:S(2)}) async-start(s8[16777216]{0:T(1024)(128)(4,1)} %bitcast.210), calls=%async_computation.20 | async-start | bytes 8388608 | tf_op jit(solution)/shard_map/while
  426.7 20.0 %slice-start.1 = ((s8[16777216]{0:T(1024)(128)(4,1)}), s8[4194304]{0:T(1024)(128)(4,1)S(1)}, s32[]{:S(2)}) async-start(s8[16777216]{0:T(1024)(128)(4,1)} %bitcast.210), calls=%async_computation.21 | async-start | bytes 8388608 | tf_op jit(solution)/shard_map/while
  464.5 98.4 %all-to-all-start.3 = ((bf16[4,1024,3,1,256]{4,0,3,2,1:T(4,128)(2,1)}), bf16[4,1024,3,1,256]{4,0,3,2,1:T(4,128)(2,1)}, u32[]{:S(2)}, u32[]{:S(2)}) async-start(bf16[4,1024,3,1,256]{4,0,3,2,1:T(4,128)(2,1)} %copy.131), calls=%async_computation.3 | async-start | bytes 12582912 | tf_op jit(solution)/shard_map/all_to_all | solution.py:170
  469.7 249.1 %reduce-scatter.13.cloned.1.call-start = ((), (), s32[]{:S(2)}) async-start(), calls=%async_computation.14 | async-start | bytes 5242880 | tf_op jit(solution)/shard_map/reduce_scatter | solution.py:185
  480.0 257.4 %reduce-scatter.9.cloned.1.call-start = ((), (), s32[]{:S(2)}) async-start(), calls=%async_computation.12 | async-start | bytes 15728640 | tf_op jit(solution)/shard_map/reduce_scatter | solution.py:184
  637.2 229.2 %reduce-scatter.17.cloned.1.call-start = ((), (), s32[]{:S(2)}) async-start(), calls=%async_computation.16 | async-start | bytes 20971520 | tf_op jit(solution)/shard_map/reduce_scatter | solution.py:186
  698.5 296.4 %reduce-scatter.21.cloned.1.call-start = ((), (), s32[]{:S(2)}) async-start(), calls=%async_computation.18 | async-start | bytes 20971520 | tf_op jit(solution)/shard_map/reduce_scatter | solution.py:187
  718.7 370.0 %reduce-scatter.15.cloned.1.call-start = ((), (), s32[]{:S(2)}) async-start(), calls=%async_computation.15 | async-start | bytes 1179648 | tf_op jit(solution)/shard_map/reduce_scatter | solution.py:191
  719.3 420.5 %reduce-scatter.11.cloned.1.call-start = ((), (), s32[]{:S(2)}) async-start(), calls=%async_computation.13 | async-start | bytes 3538944 | tf_op jit(solution)/shard_map/reduce_scatter | solution.py:190
  737.5 493.8 %reduce-scatter.19.cloned.1.call-start = ((), (), s32[]{:S(2)}) async-start(), calls=%async_computation.17 | async-start | bytes 4718592 | tf_op jit(solution)/shard_map/reduce_scatter | solution.py:192
  866.4 457.4 %reduce-scatter.23.cloned.1.call-start = ((), (), s32[]{:S(2)}) async-start(), calls=%async_computation.19 | async-start | bytes 4718592 | tf_op jit(solution)/shard_map/reduce_scatter | solution.py:193
  872.3 122.6 %copy-start.29 = (f32[1024]{0:T(1024)S(1)}, f32[1024]{0:T(1024)}, u32[]{:S(2)}) copy-start(f32[1024]{0:T(1024)} %param.24) | copy-start | bytes 12292
  (37 other events, 257.3 us)
Sparse Core Ops, SparseCore 0:
  480.1 69.5 reduce-scatter.12
  637.3 100.1 reduce-scatter.8
  740.2 126.0 reduce-scatter.16
  868.8 126.1 reduce-scatter.20
  999.1 63.3 reduce-scatter.14
  1066.6 73.1 reduce-scatter.10
  1144.0 87.2 reduce-scatter.18
  1235.9 87.7 reduce-scatter.22
